TPU v7x, 256 devices: a whole 4x4x8 slice. The times are simulated.
256 devices in a mesh: row: 16 (over z_lo, x, core), col: 16 (over y, z_hi).
Axes of the slice: x: 4, y: 4, z: 8 (z_hi: 4, z_lo: 2; z = z_hi * 2 + z_lo), core: 2. Of those that a mesh axis runs over, the one named last changes fastest.
Arguments:
- pair: bfloat16 [768, 768, 128], P('row', 'col'), may hold values from -6 to 6
- ln_gain: float32 [128], replicated, may hold values from 0.25 to 1.75
- w_query: bfloat16 [128, 128], replicated, may hold values from -46 to 46
- w_key: bfloat16 [128, 128], replicated, may hold values from -0.5 to 0.5
- w_value: bfloat16 [128, 128], replicated, may hold values from -0.5 to 0.5
- w_gate: bfloat16 [128, 128], replicated, may hold values from -0.5 to 0.5
- w_bias: bfloat16 [128, 4], replicated, may hold values from -0.5 to 0.5
- w_out: bfloat16 [128, 128], replicated, may hold values from -0.5 to 0.5
- valid_length: int32 [1], replicated, may hold values from 384 to 768
Outputs:
- update: bfloat16 [768, 768, 128], P('row', 'col')
Inputs may be any that keep to these rules, and one draw needn't show every extreme that they name: Tokens 0 to valid_length - 1 are real, the others are padding.
All inputs are finite; a program needn't handle non-finite values.
Results may differ from a plain program's by a relative error of at most 0.014.
The roundings to bfloat16 on the way count: a program that leaves them out, or rounds other values in their place, can miss the bound.
Values may be sent and summed in bfloat16 or wider, within the bound.
No kernel may reach another device: no remote copies, remote signals or barrier semaphores. Data moves between devices by JAX's collectives and lax.ppermute only.
A program may use at most 128 MiB of HBM per device.

v0:
```python
import functools
import jax
import jax.numpy as jnp
from jax import lax
from jax.experimental import pallas as pl
from jax.experimental.pallas import tpu as pltpu
from jax.sharding import Mesh, PartitionSpec as P

epsilon = 1e-05
bf16, f32 = jnp.bfloat16, jnp.float32


def contract(a, b, da, db):
    return lax.dot_general(a, b, (((da,), (db,)), ((), ())), preferred_element_type=f32)


def prepare(pair_hbm, gain_hbm, w_hbm, normed_hbm, bias_out, *refs, cuts):
    pair_ref, sems, normed_ref, normed_sems, gain_ref, w_ref, small_sems, wide_ref = refs
    rows, cols, channels = pair_ref.shape
    heads = w_ref.shape[0]
    half = cols // 2
    lanes = wide_ref.shape[1]
    runs = [pl.ds(start, stop - start) for start, stop in zip(cuts, cuts[1:])]
    fetches = [pltpu.make_async_copy(pair_hbm.at[r], pair_ref.at[r], sems.at[g]) for g, r in enumerate(runs)]
    small = [
        pltpu.make_async_copy(w_hbm, w_ref, small_sems.at[0]),
        pltpu.make_async_copy(gain_hbm, gain_ref, small_sems.at[1]),
    ]
    for fetch in fetches[:1] + small + fetches[1:]:
        fetch.start()
    for fetch in small:
        fetch.wait()
    gain = gain_ref[...]
    slots = 2 * heads
    mine = lax.axis_index("z_lo") * lax.axis_size("x") + lax.axis_index("x")

    def segment(count):
        slot = lax.broadcasted_iota(jnp.int32, (count, lanes), 1) // rows
        return lax.rem(slot + slots - mine, slots)

    own_head = lax.rem(segment(heads), heads) == lax.broadcasted_iota(jnp.int32, (heads, lanes), 0)
    wide_ref[...] = contract(w_ref[...], jnp.where(own_head, 1.0, 0.0).astype(bf16), 0, 0).astype(bf16)
    first = segment(half) < heads
    lane_j = lax.rem(lax.broadcasted_iota(jnp.int32, (half, lanes), 1), rows)
    acc = jnp.zeros((half, lanes), f32)
    stores = []
    for g, fetch in enumerate(fetches):
        fetch.wait()
        start, step = cuts[g], cuts[g + 1] - cuts[g]
        x = pair_ref[pl.ds(start, step)].reshape(step * cols, channels).astype(f32)
        centred = x - jnp.mean(x, -1, keepdims=True)
        spread = jnp.mean(centred * centred, -1, keepdims=True)
        normed = (centred * lax.rsqrt(spread + epsilon) * gain).astype(bf16)
        normed_ref[pl.ds(start, step)] = normed.reshape(step, cols, channels)
        part = pl.ds(start, step)
        stores.append(pltpu.make_async_copy(normed_ref.at[part], normed_hbm.at[part], normed_sems.at[g]))
        stores[-1].start()
        wide = contract(normed, wide_ref[...], 1, 0)
        for t in range(step):
            one = wide[t * cols : (t + 1) * cols]
            both = jnp.where(first, one[:half], one[half:])
            acc = jnp.where(lane_j == start + t, both, acc)
    bias = acc.astype(bf16)
    for c in range(bias_out.shape[0]):
        bias_out[c] = bias
    for store in stores:
        store.wait()


def deliver(source, target, sems):
    count = sems.shape[0]
    step = source.shape[0] // count
    copies = []
    for n in range(count):
        part = pl.ds(n * step, step)
        copies.append(pltpu.make_async_copy(source.at[part], target.at[part], sems.at[n]))
        copies[-1].start()
    for copy in copies:
        copy.wait()


def gate(*refs):
    refs[-1][...] = jnp.zeros_like(refs[-1])


def key_sizes(keys):
    return [keys * n // 12 for n in (8, 9, 10, 11, 12)]


def build_table(length_ref, *refs, heads, width):
    slots = len(refs) - 10
    parts_in, weights_hbm, (table, weights, parts, part_sems, sems) = refs[:slots], refs[slots : slots + 5], refs[slots + 5 :]
    _, blocks, half, queries = parts.shape
    keys = blocks * width
    x, z = lax.axis_index("x"), lax.axis_index("z_lo")
    along = lax.axis_size("x")
    places = [zz * along + lax.rem(x + by, along) for zz, by in order_of_slots(z, along)]
    fetches = [pltpu.make_async_copy(p, parts.at[q], part_sems.at[n]) for n, (p, q) in enumerate(zip(parts_in, places))]
    copies = [pltpu.make_async_copy(w, weights.at[n], sems.at[n]) for n, w in enumerate(weights_hbm)]
    for fetch in copies + fetches:
        fetch.start()
    length = length_ref[0]
    for fetch in fetches:
        fetch.wait()
    place = lax.broadcasted_iota(jnp.int32, (half, 128), 1)

    def build(c, carry):
        pieces = [parts[q, c].astype(f32) for q in range(slots)]
        for kh in range(2):
            start = pl.multiple_of(c * width + kh * half, 8)
            valid = start + lax.broadcasted_iota(jnp.int32, (half, 128), 0) < length
            for h in range(heads):
                columns = []
                for at in range(0, queries, 128):
                    inside = range(at // width, -(-(at + 128) // width))
                    value = None
                    for p in inside:
                        new = pieces[(p - kh * heads - h) % slots][:, at : at + 128]
                        value = new if value is None else jnp.where(place >= p * width - at, new, value)
                    columns.append(value)
                if kh == 1:
                    turned = [pltpu.roll(v, 64, 1) for v in columns]
                    columns = [jnp.where(place < 64, turned[(n + 1) % 3], turned[(n + 2) % 3]) for n in range(3)]
                for n, value in enumerate(columns):
                    table[h, pl.ds(start, half), n * 128 : (n + 1) * 128] = jnp.where(valid, value, -1e30)
        return carry

    sizes = key_sizes(keys)
    filled = jnp.int32(blocks)
    for used in reversed(sizes[:-1]):
        filled = jnp.where(length <= used, -(-used // width), filled)
    lax.fori_loop(0, filled, build, 0)
    for copy in copies:
        copy.wait()


def attend(length_ref, own_ref, other_ref, table, weights, passed, out_ref, *refs, heads, scale, slots):
    keys_of, values_of, queries_of, gates_of, gated_of, scores_of = [refs[n : n + 2] for n in range(0, 12, 2)]
    sides = (own_ref, other_ref)
    blocks, each, width, channels = own_ref.shape
    head = channels // heads
    keys, queries = blocks * width, slots * width
    core, x, z = lax.axis_index("core"), lax.axis_index("x"), lax.axis_index("z_lo")
    along = lax.axis_size("x")
    length = length_ref[0]
    base = (lax.axis_index("y") * lax.axis_size("z_hi") + lax.axis_index("z_hi")) * each
    bases = [(2 * (z * along + x) + near) * (each * blocks) + base for near in (core, 1 - core)]
    for ref in values_of:
        ref[:, head:] = jnp.ones_like(ref[:, head:])
    for ref in gated_of:
        ref[...] = jnp.zeros_like(ref)
    wq, wk, wo = weights[0], weights[1], weights[4]
    wv = weights[2].T
    wg = weights[3].T
    lane = lax.broadcasted_iota(jnp.int32, (width, channels), 1)
    of_head = [(lane >= h * head) & (lane < (h + 1) * head) for h in range(heads)]

    def all_rows(used):
        def cells(t, side, chosen):
            return jnp.concatenate([sides[side][c, t] for c in chosen], axis=0)

        def project_keys(t, to):
            keys_of[to][:used] = contract(cells(t, to, range(-(-used // width)))[:used], wk, 1, 0).astype(bf16)

        def project_values(t, to):
            value = contract(wv, cells(t, to, range(-(-used // width)))[:used], 1, 1).astype(bf16)
            for h in range(heads):
                values_of[to][h, :head, :used] = value[h * head : (h + 1) * head]

        def project_queries(t, to):
            asked = cells(t, to, [2 * q + core for q in range(slots)])
            query = (contract(asked, wq, 1, 0) * scale).astype(bf16)
            for h in range(heads):
                for p in range(slots):
                    q = (p - h) % slots
                    block = query[q * width : (q + 1) * width]
                    queries_of[to][h, p * width : (p + 1) * width] = jnp.where(of_head[h], block, jnp.zeros_like(block))

        def project_gates(t, to):
            asked = cells(t, to, [2 * q + core for q in range(slots)])
            gates_of[to][...] = jax.nn.sigmoid(contract(wg, asked, 1, 1)).astype(bf16).astype(f32)

        def score(at, h):
            scores = contract(keys_of[at][:used], queries_of[at][h], 1, 1) + table[h, :used]
            scores_of[h % 2][:used] = scores
            return jnp.max(scores.reshape(used // 8, 8, queries), 0)

        def blend(at, h, highest):
            exponent = jnp.exp(scores_of[h % 2][:used] - highest).astype(bf16)
            return contract(values_of[at][h, :, :used], exponent, 1, 0)

        def finish(t, at):
            update = contract(gated_of[at][...], wo, 0, 0)
            row_ok = bases[at] + t < length
            row = lax.broadcasted_iota(jnp.int32, (width, channels), 0)
            for q in range(slots):
                ok = (row + (2 * q + core) * width < length) & row_ok
                piece = update[q * width : (q + 1) * width]
                out_ref[at, q, t] = jnp.where(ok, piece, 0.0).astype(bf16)

        def one_row(at, before, following, top):
            for h in range(heads):
                highest = jnp.max(top, 0, keepdims=True)
                top = score(at, h + 1) if h + 1 < heads else score(1 - at, 0)
                total = blend(at, h, highest)
                if h == 0:
                    project_keys(following, 1 - at)
                    project_queries(following, 1 - at)
                if h == 1:
                    project_values(following, 1 - at)
                if h == 2:
                    project_gates(following, 1 - at)
                    finish(before, 1 - at)
                blended = total[:head] / total[head : head + 1]
                if h > 0:
                    blended = jnp.concatenate([blended[:, h * width :], blended[:, : h * width]], axis=1)
                part = slice(h * head, (h + 1) * head)
                gated_of[at][part] = (gates_of[at][part] * blended).astype(bf16)
            return top

        def two_rows(t, top):
            top = one_row(0, jnp.maximum(t - 1, 0), t, top)
            return one_row(1, t, jnp.minimum(t + 1, each - 1), top)

        for first in (project_keys, project_queries, project_values, project_gates):
            first(0, 0)
        lax.fori_loop(0, each, two_rows, score(0, 0))
        finish(each - 1, 1)

    sizes = key_sizes(keys)
    for n, used in enumerate(sizes):
        fits = length <= used
        if n > 0:
            fits = fits & (length > sizes[n - 1])
        pl.when(fits)(functools.partial(all_rows, used))


ROW, COL = ("z_lo", "x", "core"), ("y", "z_hi")
VMEM = pl.BlockSpec(memory_space=pltpu.VMEM)
HBM = pl.BlockSpec(memory_space=pltpu.HBM)
SMEM = pl.BlockSpec(memory_space=pltpu.SMEM)


def in_hbm(value):
    return pltpu.with_memory_space_constraint(value, pltpu.HBM)


def run_prepare(pair, ln_gain, w_bias, across):
    tile_rows, tile_cols, channels = pair.shape
    heads = w_bias.shape[1]
    half = tile_cols // 2
    lanes = 2 * heads * tile_rows
    cuts = [tile_rows * n // 6 for n in (0, 1, 6)]
    return pl.pallas_call(
        functools.partial(prepare, cuts=cuts),
        out_shape=(
            jax.ShapeDtypeStruct(pair.shape, bf16),
            jax.ShapeDtypeStruct((across, half, lanes), bf16),
        ),
        in_specs=[HBM] * 3,
        out_specs=(HBM, VMEM),
        scratch_shapes=[
            pltpu.VMEM(pair.shape, bf16),
            pltpu.SemaphoreType.DMA((len(cuts) - 1,)),
            pltpu.VMEM(pair.shape, bf16),
            pltpu.SemaphoreType.DMA((len(cuts) - 1,)),
            pltpu.VMEM((1, channels), f32),
            pltpu.VMEM((heads, channels), bf16),
            pltpu.SemaphoreType.DMA((2,)),
            pltpu.VMEM((channels, lanes), bf16),
        ],
        compiler_params=pltpu.CompilerParams(vmem_limit_bytes=16 << 20),
        name="prepare",
    )(*[in_hbm(v) for v in (pair, ln_gain.reshape(1, channels), w_bias.T)])


def order_of_slots(z, along):
    near = [(z, 0), (z, along - 1), (z, 1), (1 - z, 0)]
    return near + [(z, along - 2), (1 - z, along - 1), (1 - z, 1), (1 - z, 2)]


def run_gate(arrays):
    return pl.pallas_call(
        gate,
        out_shape=jax.ShapeDtypeStruct((8, 128), f32),
        in_specs=[HBM] * len(arrays),
        out_specs=VMEM,
        compiler_params=pltpu.CompilerParams(vmem_limit_bytes=1 << 20),
        name="gate",
    )(*arrays)


def run_build(length, parts, weights, heads, width):
    slots = len(parts)
    blocks, half, lanes = parts[0].shape
    packed = (len(weights), *weights[0].shape)
    return pl.pallas_call(
        functools.partial(build_table, heads=heads, width=width),
        out_shape=(
            jax.ShapeDtypeStruct((heads, blocks * width, slots * width), f32),
            jax.ShapeDtypeStruct(packed, bf16),
        ),
        in_specs=[SMEM] + [HBM] * (slots + len(weights)),
        out_specs=(VMEM, VMEM),
        scratch_shapes=[
            pltpu.VMEM((slots, blocks, half, lanes), bf16),
            pltpu.SemaphoreType.DMA((slots,)),
            pltpu.SemaphoreType.DMA((len(weights),)),
        ],
        compiler_params=pltpu.CompilerParams(vmem_limit_bytes=8 << 20),
        cost_estimate=pl.CostEstimate(flops=4_000_000, transcendentals=0, bytes_accessed=7_000_000),
        name="build",
    )(length, *parts, *weights)


def run_attend(length, own, other, table, weights, passed):
    _, each, width, channels = own.shape
    heads, keys, queries = table.shape
    slots = queries // width
    head = channels // heads
    return pl.pallas_call(
        functools.partial(attend, heads=heads, scale=head**-0.5, slots=slots),
        out_shape=jax.ShapeDtypeStruct((2, slots, each, width, channels), bf16),
        in_specs=[SMEM] + [VMEM] * 4 + [HBM],
        out_specs=VMEM,
        scratch_shapes=[pltpu.VMEM((keys, channels), bf16)] * 2
        + [pltpu.VMEM((heads, head + 16, keys), bf16)] * 2
        + [pltpu.VMEM((heads, queries, channels), bf16)] * 2
        + [pltpu.VMEM((channels, queries), f32)] * 2
        + [pltpu.VMEM((channels, queries), bf16)] * 2
        + [pltpu.VMEM((keys, queries), f32)] * 2,
        compiler_params=pltpu.CompilerParams(vmem_limit_bytes=20 << 20),
        cost_estimate=pl.CostEstimate(flops=2_500_000_000, transcendentals=7_000_000, bytes_accessed=4_000_000),
        name="attend",
    )(length, own, other, table, weights, passed)


def run_deliver(value):
    return pl.pallas_call(
        deliver,
        out_shape=jax.ShapeDtypeStruct(value.shape, value.dtype),
        in_specs=[VMEM],
        out_specs=HBM,
        scratch_shapes=[pltpu.SemaphoreType.DMA((6,))],
        compiler_params=pltpu.CompilerParams(vmem_limit_bytes=1 << 20),
        name="deliver",
    )(value)


def shifted(value, axis, by):
    n = lax.axis_size(axis)
    return lax.ppermute(value, axis, [(k, (k + by) % n) for k in range(n)])


def per_device_inner(pair, ln_gain, w_query, w_key, w_value, w_gate, w_bias, w_out, valid_length):
    tile_rows, tile_cols, channels = pair.shape
    heads = w_bias.shape[1]
    across = lax.axis_size(COL)
    each = tile_rows // across
    weights = [in_hbm(w) for w in (w_query, w_key, w_value, w_gate, w_out)]
    normed, bias = run_prepare(pair, ln_gain, w_bias, across)
    mine = lax.all_to_all(bias, COL, 0, 0, tiled=True)
    own = lax.all_to_all(normed.reshape(across, each, tile_cols, channels), COL, 0, 0, tiled=True)
    below = shifted(mine, "z_lo", 1)
    left = shifted(mine, "x", 1)
    right = shifted(mine, "x", -1)
    below_left = shifted(below, "x", 1)
    below_right = shifted(below, "x", -1)
    far = shifted(left, "x", 1)
    below_far = shifted(below_right, "x", -1)
    passed = run_gate([right, below_left, far, below_far])
    other = shifted(own, "core", 1)
    parts = [mine, left, right, below, far, below_left, below_right, below_far]
    table, weights = run_build(valid_length, parts, weights, heads, tile_cols)
    out = run_attend(valid_length, own, other, table, weights, passed)
    theirs = shifted(out[1], "core", 1)
    core = lax.axis_index("core")
    even = jnp.where(core == 0, out[0], theirs)
    odd = jnp.where(core == 0, theirs, out[0])
    update = jnp.stack([even, odd], axis=1).reshape(tile_rows, tile_cols, channels)
    return run_deliver(lax.all_to_all(update, COL, 0, 0, tiled=True))


def solution(mesh):
    fine = Mesh(mesh.devices.reshape(2, 4, 2, 4, 4), ROW + COL)
    placed = (P(ROW, COL, None), P(), P(), P(), P(), P(), P(), P(), P())
    return jax.shard_map(per_device_inner, mesh=fine, in_specs=placed, out_specs=P(ROW, COL, None), check_vma=False)
```

profile of v0, /device:TPU:2, one launch (start us, length us, event | category | flops | bytes accessed | tf_op | source)
XLA Modules:
  0.0 116.1 jit_solution(8832349645853742787)
XLA Ops:
  0.0 3.0 %prepare.1 = (bf16[48,48,128]{2,1,0:T(8,128)(2,1)}, bf16[16,24,384]{2,1,0:T(8,128)(2,1)S(1)}) custom-call(bf16[48,48,128]{2,1,0:T(8,128)(2,1)} %pair_hbm.1, f32[1,128]{1,0:T(1,128)} %bitcast.18, bf16[4,128]{1,0:T(4,128)(2,1)} %bitcast.17), custom_call_target="tpu_custom_call" | custom-call | tf_op jit(solution)/shard_map/prepare/pallas_call | solution.py:254
  3.0 25.0 %all_to_all.15.refs_0_ = bf16[16,24,384]{2,1,0:T(8,128)(2,1)S(1)} all-to-all(bf16[16,24,384]{2,1,0:T(8,128)(2,1)S(1)} %get-tuple-element.10), channel_id=1, replica_groups=mesh['z_lo'=2,'x'=4,'core'=2,'y'=4,'z_hi'=4] {'y','z_hi'}, dimensions={0} | all-to-all | bytes 589824 | tf_op jit(solution)/shard_map/all_to_all | solution.py:362
  28.0 3.6 %all-to-all-start = ((bf16[16,3,48,128]{3,2,1,0:T(8,128)(2,1)}), bf16[16,3,48,128]{3,2,1,0:T(8,128)(2,1)S(1)}, u32[]{:S(2)}, u32[]{:S(2)}) async-start(bf16[16,3,48,128]{3,2,1,0:T(8,128)(2,1)} %bitcast.2), calls=%async_computation | async-start | bytes 1179648 | tf_op jit(solution)/shard_map/all_to_all | solution.py:363
  31.6 1.1 collective-permute-start.3
  32.7 1.5 %collective-permute-start.1 = (bf16[16,24,384]{2,1,0:T(8,128)(2,1)S(1)}, bf16[16,24,384]{2,1,0:T(8,128)(2,1)S(1)}, u32[]{:S(2)}, u32[]{:S(2)}) collective-permute-start(bf16[16,24,384]{2,1,0:T(8,128)(2,1)S(1)} %all_to_all.15.refs_0_), channel_id=1, source_target_pairs={{0,32},{32,64},{64,96},{96,0},{1,33},{33,65},{65,97},{97,1},{2,34}... | collective-permute-start | bytes 884744 | tf_op jit(solution)/shard_map/ppermute | solution.py:352
  34.2 17.0 %collective-permute-done.3.refs_3_ = bf16[16,24,384]{2,1,0:T(8,128)(2,1)S(1)} collective-permute-done((bf16[16,24,384]{2,1,0:T(8,128)(2,1)S(1)}, bf16[16,24,384]{2,1,0:T(8,128)(2,1)S(1)}, u32[]{:S(2)}, u32[]{:S(2)}) %collective-permute-start.3) | collective-permute-done | bytes 294944 | tf_op jit(solution)/shard_map/ppermute | solution.py:352
  51.2 0.5 collective-permute-start.6
  51.8 0.6 all-to-all-done.own_ref
  52.3 0.0 collective-permute-start
  52.3 2.2 %collective-permute-start.2 = (bf16[16,24,384]{2,1,0:T(8,128)(2,1)S(1)}, bf16[16,24,384]{2,1,0:T(8,128)(2,1)S(1)}, u32[]{:S(2)}, u32[]{:S(2)}) collective-permute-start(bf16[16,24,384]{2,1,0:T(8,128)(2,1)S(1)} %all_to_all.15.refs_0_), channel_id=1, source_target_pairs={{0,96},{32,0},{64,32},{96,64},{1,97},{33,1},{65,33},{97,65},{2,98}... | collective-permute-start | bytes 884744 | tf_op jit(solution)/shard_map/ppermute | solution.py:352
  54.5 0.0 collective-permute-start.5
  54.5 0.0 collective-permute-done.1.refs_1_
  54.5 1.3 %collective-permute-start.4 = (bf16[16,24,384]{2,1,0:T(8,128)(2,1)S(1)}, bf16[16,24,384]{2,1,0:T(8,128)(2,1)S(1)}, u32[]{:S(2)}, u32[]{:S(2)}) collective-permute-start(bf16[16,24,384]{2,1,0:T(8,128)(2,1)S(1)} %collective-permute-done.1.refs_1_), channel_id=1, source_target_pairs={{0,32},{32,64},{64,96},{96,0},{1,33},{33,65},{65,97},{97,1},{2,34}... | collective-permute-start | bytes 884744 | tf_op jit(solution)/shard_map/ppermute | solution.py:352
  55.8 5.3 %collective-permute-done.6.refs_6_ = bf16[16,24,384]{2,1,0:T(8,128)(2,1)S(1)} collective-permute-done((bf16[16,24,384]{2,1,0:T(8,128)(2,1)S(1)}, bf16[16,24,384]{2,1,0:T(8,128)(2,1)S(1)}, u32[]{:S(2)}, u32[]{:S(2)}) %collective-permute-start.6) | collective-permute-done | bytes 294944 | tf_op jit(solution)/shard_map/ppermute | solution.py:352
  61.1 0.8 collective-permute-start.7
  62.6 4.9 %collective-permute-done.2.refs_2_.refs_0_ = bf16[16,24,384]{2,1,0:T(8,128)(2,1)S(1)} collective-permute-done((bf16[16,24,384]{2,1,0:T(8,128)(2,1)S(1)}, bf16[16,24,384]{2,1,0:T(8,128)(2,1)S(1)}, u32[]{:S(2)}, u32[]{:S(2)}) %collective-permute-start.2) | collective-permute-done | bytes 294944 | tf_op jit(solution)/shard_map/ppermute | solution.py:352
  67.4 0.0 collective-permute-done.5.refs_5_.refs_1_
  67.4 2.6 %collective-permute-done.4.refs_4_.refs_2_ = bf16[16,24,384]{2,1,0:T(8,128)(2,1)S(1)} collective-permute-done((bf16[16,24,384]{2,1,0:T(8,128)(2,1)S(1)}, bf16[16,24,384]{2,1,0:T(8,128)(2,1)S(1)}, u32[]{:S(2)}, u32[]{:S(2)}) %collective-permute-start.4) | collective-permute-done | bytes 294944 | tf_op jit(solution)/shard_map/ppermute | solution.py:352
  70.0 1.5 %collective-permute-done.7.refs_7_.refs_3_ = bf16[16,24,384]{2,1,0:T(8,128)(2,1)S(1)} collective-permute-done((bf16[16,24,384]{2,1,0:T(8,128)(2,1)S(1)}, bf16[16,24,384]{2,1,0:T(8,128)(2,1)S(1)}, u32[]{:S(2)}, u32[]{:S(2)}) %collective-permute-start.7) | collective-permute-done | bytes 294944 | tf_op jit(solution)/shard_map/ppermute | solution.py:352
  71.5 2.4 %build.1 = (f32[4,768,384]{2,1,0:T(8,128)S(1)}, bf16[5,128,128]{2,1,0:T(8,128)(2,1)S(1)}) custom-call(s32[1]{0:T(128)S(6)} %copy.11.length_ref, bf16[16,24,384]{2,1,0:T(8,128)(2,1)S(1)} %all_to_all.15.refs_0_, bf16[16,24,384]{2,1,0:T(8,128)(2,1)S(1)} %collective-permute-done.1.refs_1_, bf16[16,24,384]{2,1,0:T(8,128)(2,1)S(1)} %collective-permute-done.2.refs_2_.refs_0_, ...), custom_call_target="tpu_custom_call" | custom-call | flops 4000000 | bytes 7000000 | tf_op jit(solution)/shard_map/build/pallas_call | solution.py:297
  73.9 0.0 collective-permute-done.other_ref
  73.9 9.7 %attend.1 = bf16[2,8,3,48,128]{4,3,2,1,0:T(8,128)(2,1)S(1)} custom-call(s32[1]{0:T(128)S(6)} %copy.11.length_ref, bf16[16,3,48,128]{3,2,1,0:T(8,128)(2,1)S(1)} %all-to-all-done.own_ref, bf16[16,3,48,128]{3,2,1,0:T(8,128)(2,1)S(1)} %collective-permute-done.other_ref, f32[4,768,384]{2,1,0:T(8,128)S(1)} %get-tuple-element.11.table, ...), custom_call_target="tpu_custom_call" | custom-call | flops 2500000000 | bytes 4000000 | tf_op jit(solution)/shard_map/attend/pallas_call | solution.py:321
  83.7 0.1 collective-permute-start.8
  83.8 1.6 %collective-permute-done.8 = bf16[8,3,48,128]{3,2,1,0:T(8,128)(2,1)S(1)} collective-permute-done((bf16[8,3,48,128]{3,2,1,0:T(8,128)(2,1)S(1)}, bf16[8,3,48,128]{3,2,1,0:T(8,128)(2,1)S(1)}, u32[]{:S(2)}, u32[]{:S(2)}) %collective-permute-start.8) | collective-permute-done | bytes 294944 | tf_op jit(solution)/shard_map/ppermute | solution.py:352
  85.4 0.1 pad_maximum_fusion
  85.5 29.6 %all_to_all.16.source = bf16[48,48,128]{2,1,0:T(8,128)(2,1)S(1)} all-to-all(bf16[48,48,128]{2,1,0:T(8,128)(2,1)S(1)} %bitcast.16), channel_id=1, replica_groups=mesh['z_lo'=2,'x'=4,'core'=2,'y'=4,'z_hi'=4] {'y','z_hi'}, dimensions={0} | all-to-all | bytes 1179648 | tf_op jit(solution)/shard_map/all_to_all | solution.py:381
  115.1 0.9 deliver.1
  (4 shorter events, 0.1 us)
Async XLA Ops:
  28.0 24.3 %all-to-all-start = ((bf16[16,3,48,128]{3,2,1,0:T(8,128)(2,1)}), bf16[16,3,48,128]{3,2,1,0:T(8,128)(2,1)S(1)}, u32[]{:S(2)}, u32[]{:S(2)}) async-start(bf16[16,3,48,128]{3,2,1,0:T(8,128)(2,1)} %bitcast.2), calls=%async_computation | async-start | bytes 1179648 | tf_op jit(solution)/shard_map/all_to_all | solution.py:363
  31.6 19.6 %collective-permute-start.3 = (bf16[16,24,384]{2,1,0:T(8,128)(2,1)S(1)}, bf16[16,24,384]{2,1,0:T(8,128)(2,1)S(1)}, u32[]{:S(2)}, u32[]{:S(2)}) collective-permute-start(bf16[16,24,384]{2,1,0:T(8,128)(2,1)S(1)} %all_to_all.15.refs_0_), channel_id=1, source_target_pairs={{0,128},{128,0},{1,129},{129,1},{2,130},{130,2},{3,131},{131,3},{4... | collective-permute-start | bytes 884744 | tf_op jit(solution)/shard_map/ppermute | solution.py:352
  32.7 21.8 %collective-permute-start.1 = (bf16[16,24,384]{2,1,0:T(8,128)(2,1)S(1)}, bf16[16,24,384]{2,1,0:T(8,128)(2,1)S(1)}, u32[]{:S(2)}, u32[]{:S(2)}) collective-permute-start(bf16[16,24,384]{2,1,0:T(8,128)(2,1)S(1)} %all_to_all.15.refs_0_), channel_id=1, source_target_pairs={{0,32},{32,64},{64,96},{96,0},{1,33},{33,65},{65,97},{97,1},{2,34}... | collective-permute-start | bytes 884744 | tf_op jit(solution)/shard_map/ppermute | solution.py:352
  51.2 9.9 %collective-permute-start.6 = (bf16[16,24,384]{2,1,0:T(8,128)(2,1)S(1)}, bf16[16,24,384]{2,1,0:T(8,128)(2,1)S(1)}, u32[]{:S(2)}, u32[]{:S(2)}) collective-permute-start(bf16[16,24,384]{2,1,0:T(8,128)(2,1)S(1)} %collective-permute-done.3.refs_3_), channel_id=1, source_target_pairs={{0,96},{32,0},{64,32},{96,64},{1,97},{33,1},{65,33},{97,65},{2,98}... | collective-permute-start | bytes 884744 | tf_op jit(solution)/shard_map/ppermute | solution.py:352
  52.3 21.6 %collective-permute-start = (bf16[16,3,48,128]{3,2,1,0:T(8,128)(2,1)S(1)}, bf16[16,3,48,128]{3,2,1,0:T(8,128)(2,1)S(1)}, u32[]{:S(2)}, u32[]{:S(2)}) collective-permute-start(bf16[16,3,48,128]{3,2,1,0:T(8,128)(2,1)S(1)} %all-to-all-done.own_ref), channel_id=1, source_target_pairs={{0,16},{16,0},{1,17},{17,1},{2,18},{18,2},{3,19},{19,3},{4,20},{20... | collective-permute-start | bytes 1769480 | tf_op jit(solution)/shard_map/ppermute | solution.py:352
  52.3 15.1 %collective-permute-start.2 = (bf16[16,24,384]{2,1,0:T(8,128)(2,1)S(1)}, bf16[16,24,384]{2,1,0:T(8,128)(2,1)S(1)}, u32[]{:S(2)}, u32[]{:S(2)}) collective-permute-start(bf16[16,24,384]{2,1,0:T(8,128)(2,1)S(1)} %all_to_all.15.refs_0_), channel_id=1, source_target_pairs={{0,96},{32,0},{64,32},{96,64},{1,97},{33,1},{65,33},{97,65},{2,98}... | collective-permute-start | bytes 884744 | tf_op jit(solution)/shard_map/ppermute | solution.py:352
  54.5 12.9 %collective-permute-start.5 = (bf16[16,24,384]{2,1,0:T(8,128)(2,1)S(1)}, bf16[16,24,384]{2,1,0:T(8,128)(2,1)S(1)}, u32[]{:S(2)}, u32[]{:S(2)}) collective-permute-start(bf16[16,24,384]{2,1,0:T(8,128)(2,1)S(1)} %collective-permute-done.3.refs_3_), channel_id=1, source_target_pairs={{0,32},{32,64},{64,96},{96,0},{1,33},{33,65},{65,97},{97,1},{2,34}... | collective-permute-start | bytes 884744 | tf_op jit(solution)/shard_map/ppermute | solution.py:352
  54.5 15.5 %collective-permute-start.4 = (bf16[16,24,384]{2,1,0:T(8,128)(2,1)S(1)}, bf16[16,24,384]{2,1,0:T(8,128)(2,1)S(1)}, u32[]{:S(2)}, u32[]{:S(2)}) collective-permute-start(bf16[16,24,384]{2,1,0:T(8,128)(2,1)S(1)} %collective-permute-done.1.refs_1_), channel_id=1, source_target_pairs={{0,32},{32,64},{64,96},{96,0},{1,33},{33,65},{65,97},{97,1},{2,34}... | collective-permute-start | bytes 884744 | tf_op jit(solution)/shard_map/ppermute | solution.py:352
  61.1 10.4 %collective-permute-start.7 = (bf16[16,24,384]{2,1,0:T(8,128)(2,1)S(1)}, bf16[16,24,384]{2,1,0:T(8,128)(2,1)S(1)}, u32[]{:S(2)}, u32[]{:S(2)}) collective-permute-start(bf16[16,24,384]{2,1,0:T(8,128)(2,1)S(1)} %collective-permute-done.6.refs_6_), channel_id=1, source_target_pairs={{0,96},{32,0},{64,32},{96,64},{1,97},{33,1},{65,33},{97,65},{2,98}... | collective-permute-start | bytes 884744 | tf_op jit(solution)/shard_map/ppermute | solution.py:352
  83.7 1.7 %collective-permute-start.8 = (bf16[8,3,48,128]{3,2,1,0:T(8,128)(2,1)S(1)}, bf16[8,3,48,128]{3,2,1,0:T(8,128)(2,1)S(1)}, u32[]{:S(2)}, u32[]{:S(2)}) collective-permute-start(bf16[8,3,48,128]{3,2,1,0:T(8,128)(2,1)S(1)} %slice_bitcast_fusion), channel_id=1, source_target_pairs={{0,16},{16,0},{1,17},{17,1},{2,18},{18,2},{3,19},{19,3},{4,20},{20... | collective-permute-start | bytes 884744 | tf_op jit(solution)/shard_map/ppermute | solution.py:352
where the time goes:
time: 118 us; the launch traced here: 116 us
  blocking collectives  54.5 us (46%)
  waiting for transfers between devices  33.4 us (28%)
  Pallas kernels  16 us (14%)
  starting transfers between devices  11.1 us (9%)
    ppermute x9, waiting for transfers between devices, shifted(): return lax.ppermute(value, axis, [(k, (k + by) % n) for k in range(n)])  32.8 us
    all_to_all x1, blocking collectives, per_device_inner(): return run_deliver(lax.all_to_all(update, COL, 0, 0, tiled=True))  29.6 us
    all_to_all x1, blocking collectives, per_device_inner(): mine = lax.all_to_all(bias, COL, 0, 0, tiled=True)  25 us
    pallas_call x1, Pallas kernels, run_attend(): pl.pallas_call(functools.partial(attend, heads=heads, scale=head ** (-0.5...  9.73 us
    ppermute x9, starting transfers between devices, shifted(): return lax.ppermute(value, axis, [(k, (k + by) % n) for k in range(n)])  7.52 us
    all_to_all x1, starting transfers between devices, per_device_inner(): lax.all_to_all(normed.reshape(across, each, tile_cols, channels), COL, 0,...  3.58 us
    pallas_call x1, Pallas kernels, run_prepare(): pl.pallas_call(functools.partial(prepare, cuts=cuts), out_shape=(jax.Shap...  3.03 us
    pallas_call x1, Pallas kernels, run_build(): pl.pallas_call(functools.partial(build_table, heads=heads, width=width),...  2.39 us
  transfers between devices with their start and end apart: 10, of which 7 were waited for; matrix products, arithmetic and copies ran while one was open for 0% of the time, Pallas kernels for 2%

commit v1 on v0

--- a/solution.py
+++ b/solution.py
@@ -67,18 +67,6 @@
         store.wait()
 
 
-def deliver(source, target, sems):
-    count = sems.shape[0]
-    step = source.shape[0] // count
-    copies = []
-    for n in range(count):
-        part = pl.ds(n * step, step)
-        copies.append(pltpu.make_async_copy(source.at[part], target.at[part], sems.at[n]))
-        copies[-1].start()
-    for copy in copies:
-        copy.wait()
-
-
 def gate(*refs):
     refs[-1][...] = jnp.zeros_like(refs[-1])
 
@@ -335,18 +323,6 @@
     )(length, own, other, table, weights, passed)
 
 
-def run_deliver(value):
-    return pl.pallas_call(
-        deliver,
-        out_shape=jax.ShapeDtypeStruct(value.shape, value.dtype),
-        in_specs=[VMEM],
-        out_specs=HBM,
-        scratch_shapes=[pltpu.SemaphoreType.DMA((6,))],
-        compiler_params=pltpu.CompilerParams(vmem_limit_bytes=1 << 20),
-        name="deliver",
-    )(value)
-
-
 def shifted(value, axis, by):
     n = lax.axis_size(axis)
     return lax.ppermute(value, axis, [(k, (k + by) % n) for k in range(n)])
@@ -378,7 +354,7 @@
     even = jnp.where(core == 0, out[0], theirs)
     odd = jnp.where(core == 0, theirs, out[0])
     update = jnp.stack([even, odd], axis=1).reshape(tile_rows, tile_cols, channels)
-    return run_deliver(lax.all_to_all(update, COL, 0, 0, tiled=True))
+    return lax.all_to_all(update, COL, 0, 0, tiled=True)
 
 
 def solution(mesh):

time: 118 us -> 117 us (level)
  no operation moved by 1% of the time
where the time goes in v1:
time: 117 us; the launch traced here: 116 us
  blocking collectives  54.5 us (47%)
  waiting for transfers between devices  33.4 us (29%)
  Pallas kernels  15.1 us (13%)
  starting transfers between devices  11.1 us (9%)
    ppermute x9, waiting for transfers between devices, shifted(): return lax.ppermute(value, axis, [(k, (k + by) % n) for k in range(n)])  32.8 us
    all_to_all x1, blocking collectives, per_device_inner(): return lax.all_to_all(update, COL, 0, 0, tiled=True)  29.6 us
    all_to_all x1, blocking collectives, per_device_inner(): mine = lax.all_to_all(bias, COL, 0, 0, tiled=True)  25 us
    pallas_call x1, Pallas kernels, run_attend(): pl.pallas_call(functools.partial(attend, heads=heads, scale=head ** (-0.5...  9.73 us
    ppermute x9, starting transfers between devices, shifted(): return lax.ppermute(value, axis, [(k, (k + by) % n) for k in range(n)])  7.52 us
    all_to_all x1, starting transfers between devices, per_device_inner(): lax.all_to_all(normed.reshape(across, each, tile_cols, channels), COL, 0,...  3.58 us
    pallas_call x1, Pallas kernels, run_prepare(): pl.pallas_call(functools.partial(prepare, cuts=cuts), out_shape=(jax.Shap...  3.03 us
    pallas_call x1, Pallas kernels, run_build(): pl.pallas_call(functools.partial(build_table, heads=heads, width=width),...  2.39 us
  transfers between devices with their start and end apart: 10, of which 7 were waited for; matrix products, arithmetic and copies ran while one was open for 0% of the time, Pallas kernels for 2%

profile of v1, /device:TPU:2, one launch (start us, length us, event | category | flops | bytes accessed | tf_op | source)
XLA Modules:
  0.0 115.9 jit_solution(10021684896342109129)
XLA Ops:
  0.0 3.0 %prepare.1 = (bf16[48,48,128]{2,1,0:T(8,128)(2,1)}, bf16[16,24,384]{2,1,0:T(8,128)(2,1)S(1)}) custom-call(bf16[48,48,128]{2,1,0:T(8,128)(2,1)} %pair_hbm.1, f32[1,128]{1,0:T(1,128)} %bitcast.18, bf16[4,128]{1,0:T(4,128)(2,1)} %bitcast.17), custom_call_target="tpu_custom_call" | custom-call | tf_op jit(solution)/shard_map/prepare/pallas_call | solution.py:242
  3.0 25.0 %all_to_all.15.refs_0_ = bf16[16,24,384]{2,1,0:T(8,128)(2,1)S(1)} all-to-all(bf16[16,24,384]{2,1,0:T(8,128)(2,1)S(1)} %get-tuple-element.10), channel_id=1, replica_groups=mesh['z_lo'=2,'x'=4,'core'=2,'y'=4,'z_hi'=4] {'y','z_hi'}, dimensions={0} | all-to-all | bytes 589824 | tf_op jit(solution)/shard_map/all_to_all | solution.py:338
  28.0 3.6 %all-to-all-start = ((bf16[16,3,48,128]{3,2,1,0:T(8,128)(2,1)}), bf16[16,3,48,128]{3,2,1,0:T(8,128)(2,1)S(1)}, u32[]{:S(2)}, u32[]{:S(2)}) async-start(bf16[16,3,48,128]{3,2,1,0:T(8,128)(2,1)} %bitcast.2), calls=%async_computation | async-start | bytes 1179648 | tf_op jit(solution)/shard_map/all_to_all | solution.py:339
  31.6 1.1 collective-permute-start.3
  32.7 1.5 %collective-permute-start.1 = (bf16[16,24,384]{2,1,0:T(8,128)(2,1)S(1)}, bf16[16,24,384]{2,1,0:T(8,128)(2,1)S(1)}, u32[]{:S(2)}, u32[]{:S(2)}) collective-permute-start(bf16[16,24,384]{2,1,0:T(8,128)(2,1)S(1)} %all_to_all.15.refs_0_), channel_id=1, source_target_pairs={{0,32},{32,64},{64,96},{96,0},{1,33},{33,65},{65,97},{97,1},{2,34}... | collective-permute-start | bytes 884744 | tf_op jit(solution)/shard_map/ppermute | solution.py:328
  34.2 17.0 %collective-permute-done.3.refs_3_ = bf16[16,24,384]{2,1,0:T(8,128)(2,1)S(1)} collective-permute-done((bf16[16,24,384]{2,1,0:T(8,128)(2,1)S(1)}, bf16[16,24,384]{2,1,0:T(8,128)(2,1)S(1)}, u32[]{:S(2)}, u32[]{:S(2)}) %collective-permute-start.3) | collective-permute-done | bytes 294944 | tf_op jit(solution)/shard_map/ppermute | solution.py:328
  51.2 0.5 collective-permute-start.6
  51.8 0.6 all-to-all-done.own_ref
  52.3 0.0 collective-permute-start
  52.3 2.2 %collective-permute-start.2 = (bf16[16,24,384]{2,1,0:T(8,128)(2,1)S(1)}, bf16[16,24,384]{2,1,0:T(8,128)(2,1)S(1)}, u32[]{:S(2)}, u32[]{:S(2)}) collective-permute-start(bf16[16,24,384]{2,1,0:T(8,128)(2,1)S(1)} %all_to_all.15.refs_0_), channel_id=1, source_target_pairs={{0,96},{32,0},{64,32},{96,64},{1,97},{33,1},{65,33},{97,65},{2,98}... | collective-permute-start | bytes 884744 | tf_op jit(solution)/shard_map/ppermute | solution.py:328
  54.5 0.0 collective-permute-start.5
  54.5 0.0 collective-permute-done.1.refs_1_
  54.5 1.3 %collective-permute-start.4 = (bf16[16,24,384]{2,1,0:T(8,128)(2,1)S(1)}, bf16[16,24,384]{2,1,0:T(8,128)(2,1)S(1)}, u32[]{:S(2)}, u32[]{:S(2)}) collective-permute-start(bf16[16,24,384]{2,1,0:T(8,128)(2,1)S(1)} %collective-permute-done.1.refs_1_), channel_id=1, source_target_pairs={{0,32},{32,64},{64,96},{96,0},{1,33},{33,65},{65,97},{97,1},{2,34}... | collective-permute-start | bytes 884744 | tf_op jit(solution)/shard_map/ppermute | solution.py:328
  55.8 5.3 %collective-permute-done.6.refs_6_ = bf16[16,24,384]{2,1,0:T(8,128)(2,1)S(1)} collective-permute-done((bf16[16,24,384]{2,1,0:T(8,128)(2,1)S(1)}, bf16[16,24,384]{2,1,0:T(8,128)(2,1)S(1)}, u32[]{:S(2)}, u32[]{:S(2)}) %collective-permute-start.6) | collective-permute-done | bytes 294944 | tf_op jit(solution)/shard_map/ppermute | solution.py:328
  61.1 0.8 collective-permute-start.7
  62.6 4.9 %collective-permute-done.2.refs_2_.refs_0_ = bf16[16,24,384]{2,1,0:T(8,128)(2,1)S(1)} collective-permute-done((bf16[16,24,384]{2,1,0:T(8,128)(2,1)S(1)}, bf16[16,24,384]{2,1,0:T(8,128)(2,1)S(1)}, u32[]{:S(2)}, u32[]{:S(2)}) %collective-permute-start.2) | collective-permute-done | bytes 294944 | tf_op jit(solution)/shard_map/ppermute | solution.py:328
  67.4 0.0 collective-permute-done.5.refs_5_.refs_1_
  67.4 2.6 %collective-permute-done.4.refs_4_.refs_2_ = bf16[16,24,384]{2,1,0:T(8,128)(2,1)S(1)} collective-permute-done((bf16[16,24,384]{2,1,0:T(8,128)(2,1)S(1)}, bf16[16,24,384]{2,1,0:T(8,128)(2,1)S(1)}, u32[]{:S(2)}, u32[]{:S(2)}) %collective-permute-start.4) | collective-permute-done | bytes 294944 | tf_op jit(solution)/shard_map/ppermute | solution.py:328
  70.0 1.5 %collective-permute-done.7.refs_7_.refs_3_ = bf16[16,24,384]{2,1,0:T(8,128)(2,1)S(1)} collective-permute-done((bf16[16,24,384]{2,1,0:T(8,128)(2,1)S(1)}, bf16[16,24,384]{2,1,0:T(8,128)(2,1)S(1)}, u32[]{:S(2)}, u32[]{:S(2)}) %collective-permute-start.7) | collective-permute-done | bytes 294944 | tf_op jit(solution)/shard_map/ppermute | solution.py:328
  71.5 2.4 %build.1 = (f32[4,768,384]{2,1,0:T(8,128)S(1)}, bf16[5,128,128]{2,1,0:T(8,128)(2,1)S(1)}) custom-call(s32[1]{0:T(128)S(6)} %copy.12.length_ref, bf16[16,24,384]{2,1,0:T(8,128)(2,1)S(1)} %all_to_all.15.refs_0_, bf16[16,24,384]{2,1,0:T(8,128)(2,1)S(1)} %collective-permute-done.1.refs_1_, bf16[16,24,384]{2,1,0:T(8,128)(2,1)S(1)} %collective-permute-done.2.refs_2_.refs_0_, ...), custom_call_target="tpu_custom_call" | custom-call | flops 4000000 | bytes 7000000 | tf_op jit(solution)/shard_map/build/pallas_call | solution.py:285
  73.9 0.0 collective-permute-done.other_ref
  73.9 9.7 %attend.1 = bf16[2,8,3,48,128]{4,3,2,1,0:T(8,128)(2,1)S(1)} custom-call(s32[1]{0:T(128)S(6)} %copy.12.length_ref, bf16[16,3,48,128]{3,2,1,0:T(8,128)(2,1)S(1)} %all-to-all-done.own_ref, bf16[16,3,48,128]{3,2,1,0:T(8,128)(2,1)S(1)} %collective-permute-done.other_ref, f32[4,768,384]{2,1,0:T(8,128)S(1)} %get-tuple-element.11.table, ...), custom_call_target="tpu_custom_call" | custom-call | flops 2500000000 | bytes 4000000 | tf_op jit(solution)/shard_map/attend/pallas_call | solution.py:309
  83.7 0.1 collective-permute-start.8
  83.8 1.6 %collective-permute-done.8 = bf16[8,3,48,128]{3,2,1,0:T(8,128)(2,1)S(1)} collective-permute-done((bf16[8,3,48,128]{3,2,1,0:T(8,128)(2,1)S(1)}, bf16[8,3,48,128]{3,2,1,0:T(8,128)(2,1)S(1)}, u32[]{:S(2)}, u32[]{:S(2)}) %collective-permute-start.8) | collective-permute-done | bytes 294944 | tf_op jit(solution)/shard_map/ppermute | solution.py:328
  85.4 0.1 pad_maximum_fusion
  85.5 29.6 %all_to_all.16 = bf16[48,48,128]{2,1,0:T(8,128)(2,1)S(1)} all-to-all(bf16[48,48,128]{2,1,0:T(8,128)(2,1)S(1)} %bitcast.16), channel_id=1, replica_groups=mesh['z_lo'=2,'x'=4,'core'=2,'y'=4,'z_hi'=4] {'y','z_hi'}, dimensions={0} | all-to-all | bytes 1179648 | tf_op jit(solution)/shard_map/all_to_all | solution.py:357
  115.1 0.8 copy.13
  (4 shorter events, 0.1 us)
Async XLA Ops:
  28.0 24.3 %all-to-all-start = ((bf16[16,3,48,128]{3,2,1,0:T(8,128)(2,1)}), bf16[16,3,48,128]{3,2,1,0:T(8,128)(2,1)S(1)}, u32[]{:S(2)}, u32[]{:S(2)}) async-start(bf16[16,3,48,128]{3,2,1,0:T(8,128)(2,1)} %bitcast.2), calls=%async_computation | async-start | bytes 1179648 | tf_op jit(solution)/shard_map/all_to_all | solution.py:339
  31.6 19.6 %collective-permute-start.3 = (bf16[16,24,384]{2,1,0:T(8,128)(2,1)S(1)}, bf16[16,24,384]{2,1,0:T(8,128)(2,1)S(1)}, u32[]{:S(2)}, u32[]{:S(2)}) collective-permute-start(bf16[16,24,384]{2,1,0:T(8,128)(2,1)S(1)} %all_to_all.15.refs_0_), channel_id=1, source_target_pairs={{0,128},{128,0},{1,129},{129,1},{2,130},{130,2},{3,131},{131,3},{4... | collective-permute-start | bytes 884744 | tf_op jit(solution)/shard_map/ppermute | solution.py:328
  32.7 21.8 %collective-permute-start.1 = (bf16[16,24,384]{2,1,0:T(8,128)(2,1)S(1)}, bf16[16,24,384]{2,1,0:T(8,128)(2,1)S(1)}, u32[]{:S(2)}, u32[]{:S(2)}) collective-permute-start(bf16[16,24,384]{2,1,0:T(8,128)(2,1)S(1)} %all_to_all.15.refs_0_), channel_id=1, source_target_pairs={{0,32},{32,64},{64,96},{96,0},{1,33},{33,65},{65,97},{97,1},{2,34}... | collective-permute-start | bytes 884744 | tf_op jit(solution)/shard_map/ppermute | solution.py:328
  51.2 9.9 %collective-permute-start.6 = (bf16[16,24,384]{2,1,0:T(8,128)(2,1)S(1)}, bf16[16,24,384]{2,1,0:T(8,128)(2,1)S(1)}, u32[]{:S(2)}, u32[]{:S(2)}) collective-permute-start(bf16[16,24,384]{2,1,0:T(8,128)(2,1)S(1)} %collective-permute-done.3.refs_3_), channel_id=1, source_target_pairs={{0,96},{32,0},{64,32},{96,64},{1,97},{33,1},{65,33},{97,65},{2,98}... | collective-permute-start | bytes 884744 | tf_op jit(solution)/shard_map/ppermute | solution.py:328
  52.3 21.6 %collective-permute-start = (bf16[16,3,48,128]{3,2,1,0:T(8,128)(2,1)S(1)}, bf16[16,3,48,128]{3,2,1,0:T(8,128)(2,1)S(1)}, u32[]{:S(2)}, u32[]{:S(2)}) collective-permute-start(bf16[16,3,48,128]{3,2,1,0:T(8,128)(2,1)S(1)} %all-to-all-done.own_ref), channel_id=1, source_target_pairs={{0,16},{16,0},{1,17},{17,1},{2,18},{18,2},{3,19},{19,3},{4,20},{20... | collective-permute-start | bytes 1769480 | tf_op jit(solution)/shard_map/ppermute | solution.py:328
  52.3 15.1 %collective-permute-start.2 = (bf16[16,24,384]{2,1,0:T(8,128)(2,1)S(1)}, bf16[16,24,384]{2,1,0:T(8,128)(2,1)S(1)}, u32[]{:S(2)}, u32[]{:S(2)}) collective-permute-start(bf16[16,24,384]{2,1,0:T(8,128)(2,1)S(1)} %all_to_all.15.refs_0_), channel_id=1, source_target_pairs={{0,96},{32,0},{64,32},{96,64},{1,97},{33,1},{65,33},{97,65},{2,98}... | collective-permute-start | bytes 884744 | tf_op jit(solution)/shard_map/ppermute | solution.py:328
  54.5 12.9 %collective-permute-start.5 = (bf16[16,24,384]{2,1,0:T(8,128)(2,1)S(1)}, bf16[16,24,384]{2,1,0:T(8,128)(2,1)S(1)}, u32[]{:S(2)}, u32[]{:S(2)}) collective-permute-start(bf16[16,24,384]{2,1,0:T(8,128)(2,1)S(1)} %collective-permute-done.3.refs_3_), channel_id=1, source_target_pairs={{0,32},{32,64},{64,96},{96,0},{1,33},{33,65},{65,97},{97,1},{2,34}... | collective-permute-start | bytes 884744 | tf_op jit(solution)/shard_map/ppermute | solution.py:328
  54.5 15.5 %collective-permute-start.4 = (bf16[16,24,384]{2,1,0:T(8,128)(2,1)S(1)}, bf16[16,24,384]{2,1,0:T(8,128)(2,1)S(1)}, u32[]{:S(2)}, u32[]{:S(2)}) collective-permute-start(bf16[16,24,384]{2,1,0:T(8,128)(2,1)S(1)} %collective-permute-done.1.refs_1_), channel_id=1, source_target_pairs={{0,32},{32,64},{64,96},{96,0},{1,33},{33,65},{65,97},{97,1},{2,34}... | collective-permute-start | bytes 884744 | tf_op jit(solution)/shard_map/ppermute | solution.py:328
  61.1 10.4 %collective-permute-start.7 = (bf16[16,24,384]{2,1,0:T(8,128)(2,1)S(1)}, bf16[16,24,384]{2,1,0:T(8,128)(2,1)S(1)}, u32[]{:S(2)}, u32[]{:S(2)}) collective-permute-start(bf16[16,24,384]{2,1,0:T(8,128)(2,1)S(1)} %collective-permute-done.6.refs_6_), channel_id=1, source_target_pairs={{0,96},{32,0},{64,32},{96,64},{1,97},{33,1},{65,33},{97,65},{2,98}... | collective-permute-start | bytes 884744 | tf_op jit(solution)/shard_map/ppermute | solution.py:328
  83.7 1.7 %collective-permute-start.8 = (bf16[8,3,48,128]{3,2,1,0:T(8,128)(2,1)S(1)}, bf16[8,3,48,128]{3,2,1,0:T(8,128)(2,1)S(1)}, u32[]{:S(2)}, u32[]{:S(2)}) collective-permute-start(bf16[8,3,48,128]{3,2,1,0:T(8,128)(2,1)S(1)} %slice_bitcast_fusion), channel_id=1, source_target_pairs={{0,16},{16,0},{1,17},{17,1},{2,18},{18,2},{3,19},{19,3},{4,20},{20... | collective-permute-start | bytes 884744 | tf_op jit(solution)/shard_map/ppermute | solution.py:328
